TPU v7x, 32 devices: a whole 2x2x4 slice. The times are simulated.
32 devices in a mesh: gx: 4 (over x, core), gy: 8 (over z, y).
Axes of the slice: x: 2, y: 2, z: 4, core: 2. Of those that a mesh axis runs over, the one named last changes fastest.
Arguments:
- queries: bfloat16 [256, 2560], P('gx'), may hold values from -8 to 8
- token_key_value: bfloat16 [256, 1024], P('gx'), may hold values from -6 to 6
- group_cached_keys: bfloat16 [4, 32768, 512], P('gx', 'gy'), may hold values from -8 to 8
- group_cached_values: bfloat16 [4, 32768, 512], P('gx', 'gy'), may hold values from -6 to 6
- owners: int32 [4, 32768], P('gx', 'gy'), may hold values from 0 to 63, never falling along the last dimension, each value on 1 to 16384 neighbouring positions
- out_weight: bfloat16 [2560, 2560], P(None, 'gy'), may hold values from -0.125 to 0.125
- residual: bfloat16 [256, 2560], P('gx', 'gy'), may hold values from -6 to 6
- norm_gain: bfloat16 [2560], P('gy'), may hold values from 0.099609375 to 1.8984375
- expert_ids: int32 [256, 6], replicated, may hold values from 0 to 63, all different within a row; in each aligned block of 64 rows (0 to 63, 64 to 127, ...) at most 12 rows name the same one
- gate_logits: float32 [256, 6], replicated, may hold values from -0.5 to 0.5
- w_gate_up: bfloat16 [64, 2560, 3072], P('gx', 'gy'), may hold values from -0.125 to 0.125
- w_down: bfloat16 [64, 1536, 2560], P('gx', None, 'gy'), may hold values from -0.15625 to 0.15625
Outputs:
- layer_out: float32 [256, 2560], P('gx', 'gy')
Inputs may be any that keep to these rules, and one draw needn't show every extreme that they name: `owners`: each request's positions form one run; every request owns at least one position and at most 16384, and some request owns exactly 16384. `expert_ids`: within each group of 64 requests no expert is named by more than 12 requests, a bound that some block reaches.
All inputs are finite; a program needn't handle non-finite values.
Results may differ from a plain program's by a relative error of at most 0.0075.
Values may be sent and summed in bfloat16 or wider, within the bound.
No kernel may reach another device: no remote copies, remote signals or barrier semaphores. Data moves between devices by JAX's collectives and lax.ppermute only.
A program may use at most 192 MiB of HBM per device.

v0:
```python
import jax
import jax.numpy as jnp
from jax import lax
from jax.sharding import PartitionSpec as P

D = 2560
QUERY_HEADS = 20
KEY_VALUE_HEADS = 4
HEAD_SIZE = 128
E = 64
TOPK = 6
CAPS = 12
minimal_score = -1e30
norm_epsilon = 1e-05


def merged(part, axis, combine):
    gathered = jax.tree.map(lambda a: lax.all_gather(a, axis), part)

    def take(source):
        return jax.tree.map(lambda a: lax.dynamic_index_in_dim(a, source, 0, False), gathered)

    return lax.fori_loop(
        1, lax.axis_size(axis), lambda source, state: combine(state, take(source)), take(0)
    )


def merge_partial(earlier_part, later_part):
    max_one, den_one, acc_one = earlier_part
    max_two, den_two, acc_two = later_part
    peak = jnp.maximum(max_one, max_two)
    scale_one = jnp.exp(max_one - peak)
    scale_two = jnp.exp(max_two - peak)
    return (
        peak,
        den_one * scale_one + den_two * scale_two,
        acc_one * scale_one[..., None] + acc_two * scale_two[..., None],
    )


def slot_ranks(flat_ids, num_experts):
    onehot = (flat_ids[..., None] == lax.iota(jnp.int32, num_experts)).astype(jnp.int32)
    earlier = jnp.cumsum(onehot, axis=-2) - onehot
    return jnp.sum(earlier * onehot, axis=-1)


def attend_local(queries, group_cached_keys, group_cached_values, owners):
    request_rows = queries.shape[0]
    query_heads_per_group = QUERY_HEADS // KEY_VALUE_HEADS
    positions = group_cached_keys.shape[0]
    block_length = min(positions, 512)
    block_count = positions // block_length
    key_block_list = group_cached_keys.reshape(
        block_count, block_length, KEY_VALUE_HEADS, HEAD_SIZE
    )
    value_block_list = group_cached_values.reshape(
        block_count, block_length, KEY_VALUE_HEADS, HEAD_SIZE
    )
    owner_blocks = owners.reshape(block_count, block_length)
    scaling = HEAD_SIZE ** (-0.5)
    request_ids = lax.iota(jnp.int32, request_rows)

    def visit_block(state_in, inputs):
        run_max, run_den, run_acc = state_in
        key_block, value_block, owning_block = inputs
        picked_experts = queries[owning_block].reshape(
            block_length, KEY_VALUE_HEADS, query_heads_per_group, HEAD_SIZE
        )
        scores = (
            jnp.einsum(
                "tkgd,tkd->tkg", picked_experts, key_block, preferred_element_type=jnp.float32
            )
            * scaling
        )
        member = owning_block[:, None] == request_ids[None, :]
        block_max = jnp.max(
            jnp.where(member[:, :, None, None], scores[:, None], minimal_score), axis=0
        )
        new_max = jnp.maximum(run_max, block_max)
        prob_block = jnp.exp(scores - new_max[owning_block]).astype(jnp.bfloat16)
        spread = jnp.where(
            member[:, :, None, None], prob_block[:, None], jnp.zeros((), jnp.bfloat16)
        )
        rescale = jnp.exp(run_max - new_max)
        run_den = run_den * rescale + jnp.sum(spread.astype(jnp.float32), axis=0)
        run_acc = run_acc * rescale[..., None] + jnp.einsum(
            "trkg,tkd->rkgd", spread, value_block, preferred_element_type=jnp.float32
        )
        return ((new_max, run_den, run_acc), None)

    initial = (
        jnp.full(
            (request_rows, KEY_VALUE_HEADS, query_heads_per_group), minimal_score, jnp.float32
        ),
        jnp.zeros((request_rows, KEY_VALUE_HEADS, query_heads_per_group), jnp.float32),
        jnp.zeros((request_rows, KEY_VALUE_HEADS, query_heads_per_group, HEAD_SIZE), jnp.float32),
    )
    return lax.scan(visit_block, initial, (key_block_list, value_block_list, owner_blocks))[0]


def expert_block(tokens, w_gate_up, w_down):
    hidden_units = w_down.shape[1]
    gate_up = jnp.einsum("sekd,edf->sekf", tokens, w_gate_up, preferred_element_type=jnp.float32)
    gate_up = lax.psum(gate_up, "gy")
    active = (jax.nn.silu(gate_up[..., :hidden_units]) * gate_up[..., hidden_units:]).astype(
        jnp.bfloat16
    )
    return jnp.einsum("sekf,efd->sekd", active, w_down, preferred_element_type=jnp.float32).astype(
        jnp.bfloat16
    )


def shards(
    queries,
    token_key_value,
    group_cached_keys,
    group_cached_values,
    owners,
    out_weight,
    residual,
    norm_gain,
    expert_ids,
    gate_logits,
    w_gate_up,
    w_down,
):
    request_rows = queries.shape[0]
    query_heads_per_group = QUERY_HEADS // KEY_VALUE_HEADS
    key_value_width = token_key_value.shape[1] // 2
    scaling = HEAD_SIZE ** (-0.5)
    run_max, run_den, run_acc = attend_local(
        queries, group_cached_keys[0], group_cached_values[0], owners[0]
    )
    query_head_rows = queries.reshape(
        request_rows, KEY_VALUE_HEADS, query_heads_per_group, HEAD_SIZE
    )
    appended_keys = token_key_value[:, :key_value_width].reshape(
        request_rows, KEY_VALUE_HEADS, HEAD_SIZE
    )
    appended_values = token_key_value[:, key_value_width:]
    own_score = (
        jnp.einsum(
            "rkgd,rkd->rkg", query_head_rows, appended_keys, preferred_element_type=jnp.float32
        )
        * scaling
    )
    run_max, run_den, run_acc = merged((run_max, run_den, run_acc), "gy", merge_partial)
    peak = jnp.maximum(run_max, own_score)
    rescale = jnp.exp(run_max - peak)
    own_prob = lax.optimization_barrier(jnp.exp(own_score - peak).astype(jnp.bfloat16)).astype(
        jnp.float32
    )
    denominator = run_den * rescale + own_prob
    incoming_values = appended_values.astype(jnp.float32).reshape(
        request_rows, KEY_VALUE_HEADS, 1, HEAD_SIZE
    )
    numerator = run_acc * rescale[..., None] + own_prob[..., None] * incoming_values
    attention = (
        (numerator / denominator[..., None])
        .astype(jnp.bfloat16)
        .reshape(request_rows, QUERY_HEADS * HEAD_SIZE)
    )
    projected = jnp.dot(attention, out_weight, preferred_element_type=jnp.float32)
    hidden = (residual.astype(jnp.float32) + projected).astype(jnp.bfloat16)
    hidden_f = hidden.astype(jnp.float32)
    squares = lax.psum(jnp.sum(hidden_f * hidden_f, axis=1), "gy")
    inv_rms = lax.rsqrt(squares / D + norm_epsilon)
    normed = (hidden_f * inv_rms[:, None] * norm_gain.astype(jnp.float32)[None, :]).astype(
        jnp.bfloat16
    )
    mixing = jax.nn.softmax(gate_logits, axis=-1)
    num_gx = lax.axis_size("gx")
    group_index = lax.axis_index("gx")
    per_row = w_gate_up.shape[0]
    columns_here = normed.shape[1]
    my_ids = lax.dynamic_slice_in_dim(
        expert_ids, group_index * request_rows, request_rows, 0
    ).reshape(-1)
    my_mix = lax.dynamic_slice_in_dim(mixing, group_index * request_rows, request_rows, 0)
    places = my_ids * CAPS + slot_ranks(my_ids, E)
    outgoing = (
        jnp.zeros((E * CAPS, columns_here), jnp.bfloat16)
        .at[places]
        .set(jnp.repeat(normed, TOPK, axis=0))
    )
    returned = lax.all_to_all(
        expert_block(
            lax.all_to_all(
                outgoing.reshape(num_gx, per_row, CAPS, columns_here),
                "gx",
                split_axis=0,
                concat_axis=0,
                tiled=True,
            ),
            w_gate_up,
            w_down,
        ),
        "gx",
        split_axis=0,
        concat_axis=0,
        tiled=True,
    )
    picked = (
        returned.reshape(E * CAPS, columns_here)[places]
        .astype(jnp.float32)
        .reshape(request_rows, TOPK, columns_here)
    )
    routed = jnp.sum(my_mix[..., None] * picked, axis=1)
    return hidden_f + routed


def solution(mesh):
    placed = (
        P("gx", None),
        P("gx", None),
        P("gx", "gy", None),
        P("gx", "gy", None),
        P("gx", "gy"),
        P(None, "gy"),
        P("gx", "gy"),
        P("gy"),
        P(),
        P(),
        P("gx", "gy", None),
        P("gx", None, "gy"),
    )
    return jax.shard_map(
        shards, mesh=mesh, in_specs=placed, out_specs=P("gx", "gy"), check_vma=False
    )
```

profile of v0, /device:TPU:0, one launch (start us, length us, event | category | flops | bytes accessed | tf_op | source)
XLA Modules:
  0.0 817.4 jit_solution(4890092526414652480)
XLA Ops:
  6.5 7.0 reshape.208
  13.6 7.0 reshape_squeeze.10
  22.4 178.0 %while.35 = (s32[]{:T(128)}, f32[64,4,5]{2,1,0:T(4,128)S(1)}, f32[64,4,5]{2,1,0:T(4,128)S(1)}, f32[64,4,5,128]{3,0,2,1:T(8,128)}, s32[8,512]{1,0:T(8,128)}, /*in...) while((s32[]{:T(128)}, f32[64,4,5]{2,1,0:T(4,128)S(1)}, ...), condition=%wide.region_3.4_spmd.clone, body=%wide.region_0.3_spmd.clone.sunk | while | flops 176462592 | bytes 21555320 | solution.py:98
  23.1 3.6 gather_fusion
  26.7 4.5 copy.169
  31.2 2.1 bitcast_convert_fusion.2
  34.9 2.3 multiply_reduce_fusion.4
  37.8 2.1 gather_fusion.1
  44.4 3.6 gather_fusion
  48.0 4.5 copy.169
  52.5 2.1 bitcast_convert_fusion.2
  56.2 2.3 multiply_reduce_fusion.4
  59.1 2.1 gather_fusion.1
  63.6 2.4 fusion.70
  66.8 3.6 gather_fusion
  70.4 4.5 copy.169
  74.9 2.1 bitcast_convert_fusion.2
  78.6 2.3 multiply_reduce_fusion.4
  81.5 2.1 gather_fusion.1
  86.0 2.4 fusion.70
  89.2 3.6 gather_fusion
  92.8 4.5 copy.169
  97.3 2.1 bitcast_convert_fusion.2
  101.0 2.3 multiply_reduce_fusion.4
  103.9 2.1 gather_fusion.1
  108.4 2.4 fusion.70
  111.6 3.6 gather_fusion
  115.2 4.5 copy.169
  119.7 2.1 bitcast_convert_fusion.2
  123.4 2.3 multiply_reduce_fusion.4
  126.3 2.1 gather_fusion.1
  130.8 2.4 fusion.70
  134.0 3.6 gather_fusion
  137.6 4.5 copy.169
  142.1 2.1 bitcast_convert_fusion.2
  145.8 2.3 multiply_reduce_fusion.4
  148.7 2.1 gather_fusion.1
  153.2 2.4 fusion.70
  156.4 3.6 gather_fusion
  160.0 4.5 copy.169
  164.5 2.1 bitcast_convert_fusion.2
  168.1 2.3 multiply_reduce_fusion.4
  171.1 2.1 gather_fusion.1
  175.6 2.4 fusion.70
  178.8 3.6 gather_fusion
  182.4 4.5 copy.169
  186.8 2.1 bitcast_convert_fusion.2
  190.5 2.3 multiply_reduce_fusion.4
  193.5 2.1 gather_fusion.1
  198.0 2.4 fusion.70
  202.2 38.6 %all-gather = f32[512,4,5]{2,1,0:T(4,128)S(1)} all-gather(f32[64,4,5]{2,1,0:T(4,128)S(1)} %get-tuple-element.232), channel_id=2, replica_groups=mesh['gx'=4,'gy'=8] {'gy'}, dimensions={0}, use_global_device_ids=true | all-gather | bytes 46080 | tf_op jit(solution)/shard_map/all_gather | solution.py:18
  240.9 35.2 %all-gather.1 = f32[512,4,5]{2,1,0:T(4,128)S(1)} all-gather(f32[64,4,5]{2,1,0:T(4,128)S(1)} %get-tuple-element.233), channel_id=3, replica_groups=mesh['gx'=4,'gy'=8] {'gy'}, dimensions={0}, use_global_device_ids=true | all-gather | bytes 46080 | tf_op jit(solution)/shard_map/all_gather | solution.py:18
  282.6 27.2 %all-gather.5.cloned.1.call-done = f32[512,4,5,128]{3,0,2,1:T(8,128)} async-done(((f32[64,4,5,128]{3,0,2,1:T(8,128)}), f32[512,4,5,128]{3,0,2,1:T(8,128)}) %all-gather.5.cloned.1.call-update) | async-done | bytes 5242896 | tf_op jit(solution)/shard_map/all_gather | solution.py:18
  311.4 20.6 %while.34 = (s32[]{:T(128)}, f32[64,4,5]{0,1,2:T(4,128)S(1)}, f32[64,4,5]{0,1,2:T(4,128)S(1)}, f32[64,4,5,128]{3,2,1,0:T(8,128)S(1)}, f32[8,64,4,5]{1,2,3,0:T(4,...) while((s32[]{:T(128)}, f32[64,4,5]{0,1,2:T(4,128)S(1)}, ...), condition=%wide.region_5.6_spmd, body=%wide.region_4.5_spmd.sunk | while | flops 499205 | bytes 3348631 | solution.py:23
  333.7 1.9 divide_convert_fusion
  336.7 19.3 %psum.14 = f32[64]{0:T(128)S(1)} all-reduce(f32[64]{0:T(128)S(1)} %get-tuple-element.365), channel_id=1, replica_groups=mesh['gx'=4,'gy'=8] {'gy'}, use_global_device_ids=true, to_apply=%region_12.13 | all-reduce | flops 64 | bytes 512 | tf_op jit(solution)/shard_map/psum | solution.py:166
  356.3 2.1 scatter_custom_fusion
  358.7 12.1 %all_to_all.10 = bf16[4,16,12,320]{3,1,2,0:T(8,128)(2,1)S(1)} all-to-all(bf16[4,16,12,320]{3,1,2,0:T(8,128)(2,1)S(1)} %copy.108), channel_id=1, replica_groups=mesh['gx'=4,'gy'=8] {'gx'}, dimensions={0} | all-to-all | bytes 983040 | tf_op jit(solution)/shard_map/all_to_all | solution.py:188
  370.8 16.6 %fusion.23 = f32[4,16,12,3072]{3,2,0,1:T(8,128)} fusion(bf16[16,320,3072]{2,1,0:T(8,128)(2,1)} %param.26, bf16[4,16,12,320]{3,1,2,0:T(8,128)(2,1)S(1)} %all_to_all.10), kind=kOutput, calls=%fused_computation.44 | convolution fusion | flops 1509949440 | bytes 41385984 | tf_op jit(solution)/shard_map/sekd,edf->sekf/dot_general | solution.py:103
  388.2 393.0 %all-reduce.2.cloned.1.call-done = f32[4,16,12,3072]{3,2,0,1:T(8,128)} async-done(((f32[4,16,12,3072]{3,2,0,1:T(8,128)}), f32[4,16,12,3072]{3,2,0,1:T(8,128)}) %all-reduce.2.cloned.1.call-update) | async-done | bytes 9437200 | tf_op jit(solution)/shard_map/psum | solution.py:104
  781.2 11.6 %fusion.34 = bf16[4,16,12,320]{3,2,0,1:T(8,128)(2,1)S(1)} fusion(bf16[16,1536,320]{1,2,0:T(8,128)(2,1)} %param.27, f32[4,16,12,3072]{3,2,0,1:T(8,128)} %all-reduce.2.cloned.1.call-done), kind=kOutput, calls=%fused_computation.49 | convolution fusion | flops 762298368 | bytes 25657344 | tf_op jit(solution)/shard_map/sekf,efd->sekd/dot_general | solution.py:108
  793.9 3.5 all-to-all-start.1
  797.7 9.2 %all-to-all-done.1 = bf16[4,16,12,320]{3,1,2,0:T(8,128)(2,1)S(1)} async-done(((bf16[4,16,12,320]{3,1,2,0:T(8,128)(2,1)}), bf16[4,16,12,320]{3,1,2,0:T(8,128)(2,1)S(1)}, u32[]{:S(2)}, u32[]{:S(2)}) %all-to-all-start.1) | async-done | bytes 491552 | tf_op jit(solution)/shard_map/all_to_all | solution.py:186
  807.4 2.1 gather_fusion.2
  (260 shorter events, 82.1 us)
Async XLA Ops:
  6.5 329.4 %copy-start = (bf16[2560,320]{0,1:T(8,128)(2,1)S(1)}, bf16[2560,320]{0,1:T(8,128)(2,1)}, u32[]{:S(2)}) copy-start(bf16[2560,320]{0,1:T(8,128)(2,1)} %param.21) | copy-start | bytes 4915204
  6.5 303.3 %all-gather.5.cloned.1.call-start = ((), (), s32[]{:S(2)}) async-start(), calls=%async_computation.3 | async-start | bytes 5898240 | tf_op jit(solution)/shard_map/all_gather | solution.py:18
  13.6 7.5 copy-start.6
  13.6 8.8 %copy-start.1 = (bf16[64,2560]{1,0:T(8,128)(2,1)S(1)}, bf16[64,2560]{1,0:T(8,128)(2,1)}, u32[]{:S(2)}) copy-start(bf16[64,2560]{1,0:T(8,128)(2,1)} %param.16) | copy-start | bytes 983044
  22.4 179.4 %copy-start.7 = (s32[256,6]{0,1:T(8,128)S(1)}, s32[256,6]{0,1:T(8,128)}, u32[]{:S(2)}) copy-start(s32[256,6]{0,1:T(8,128)} %param.24) | copy-start | bytes 18436
  200.4 78.9 %copy-start.3 = (bf16[64,1024]{1,0:T(8,128)(2,1)S(1)}, bf16[64,1024]{1,0:T(8,128)(2,1)}, u32[]{:S(2)}) copy-start(bf16[64,1024]{1,0:T(8,128)(2,1)} %param.17) | copy-start | bytes 393220
  200.5 80.5 %copy-start.8 = (bf16[320]{0:T(512)(128)(2,1)S(1)}, bf16[320]{0:T(512)(128)(2,1)}, u32[]{:S(2)}) copy-start(bf16[320]{0:T(512)(128)(2,1)} %param.23) | copy-start | bytes 1924
  200.5 580.7 %all-reduce.2.cloned.1.call-start = ((), (), s32[]{:S(2)}) async-start(), calls=%async_computation.2 | async-start | bytes 25165824 | tf_op jit(solution)/shard_map/psum | solution.py:104
  276.2 1.0 copy-start.2
  311.4 24.6 %copy-start.4 = (bf16[64,320]{1,0:T(8,128)(2,1)S(1)}, bf16[64,320]{1,0:T(8,128)(2,1)}, u32[]{:S(2)}) copy-start(bf16[64,320]{1,0:T(8,128)(2,1)} %param.22) | copy-start | bytes 122884
  387.4 0.7 copy-start.5
  793.9 13.0 %all-to-all-start.1 = ((bf16[4,16,12,320]{3,1,2,0:T(8,128)(2,1)}), bf16[4,16,12,320]{3,1,2,0:T(8,128)(2,1)S(1)}, u32[]{:S(2)}, u32[]{:S(2)}) async-start(bf16[4,16,12,320]{3,1,2,0:T(8,128)(2,1)} %copy.110), calls=%async_computation.1 | async-start | bytes 1179648 | tf_op jit(solution)/shard_map/all_to_all | solution.py:186
Sparse Core Ops, SparseCore 0:
  200.6 109.1 all-gather.4
  387.6 393.5 all-reduce.1
where the time goes:
time: 821 us; the launch traced here: 817 us
  waiting for transfers between devices  429 us (52%)
  local copies, waits for them, and re-layouts  151 us (18%)
  blocking collectives  105 us (13%)
  other arithmetic  64.6 us (8%)
  matrix products  48.9 us (6%)
  between operations  13.7 us (2%)
    psum x1, waiting for transfers between devices, expert_block(): gate_up = lax.psum(gate_up, 'gy')  393 us
    all_gather x2, blocking collectives, merged(): gathered = jax.tree.map(lambda a: lax.all_gather(a, axis), part)  73.9 us
    while x24, local copies, waits for them, and re-layouts  48.4 us
    while x16, other arithmetic  35.7 us
    gather x8, local copies, waits for them, and re-layouts, visit_block(): queries[owning_block]  28.5 us
    all_gather x1, waiting for transfers between devices, merged(): gathered = jax.tree.map(lambda a: lax.all_gather(a, axis), part)  27.2 us
    gather x16, local copies, waits for them, and re-layouts, visit_block(): prob_block = jnp.exp(scores - new_max[owning_block]).astype(jnp.bfloat16)  19.4 us
    psum x1, blocking collectives, shards(): squares = lax.psum(jnp.sum(hidden_f * hidden_f, axis=1), 'gy')  19.3 us
  transfers between devices with their start and end apart: 3, of which 3 were waited for; matrix products, arithmetic and copies ran while one was open for 1% of the time, Pallas kernels for 0%

commit v1 on v0

--- a/solution.py
+++ b/solution.py
@@ -101,7 +101,7 @@
 def expert_block(tokens, w_gate_up, w_down):
     hidden_units = w_down.shape[1]
     gate_up = jnp.einsum("sekd,edf->sekf", tokens, w_gate_up, preferred_element_type=jnp.float32)
-    gate_up = lax.psum(gate_up, "gy")
+    gate_up = jnp.sum(lax.all_gather(gate_up, "gy"), axis=0)
     active = (jax.nn.silu(gate_up[..., :hidden_units]) * gate_up[..., hidden_units:]).astype(
         jnp.bfloat16
     )

time: 821 us -> 2360 us (2.87)
  waiting for transfers between devices: 429 us -> 1930 us
  other arithmetic: 64.6 us -> 101 us
    all_gather x0 -> x1, waiting for transfers between devices: none -> 1890 us  [expert_block(): gate_up = jnp.sum(lax.all_gather(gate_up, 'gy'), axis=0)]
    psum x1 -> x0, waiting for transfers between devices: 393 us -> none  [expert_block(): gate_up = lax.psum(gate_up, 'gy')]
    reduce_sum x0 -> x1, other arithmetic: none -> 36.1 us  [expert_block(): gate_up = jnp.sum(lax.all_gather(gate_up, 'gy'), axis=0)]
  transfers between devices with their start and end apart: 3 -> 3, of which waited for: 3 -> 3; matrix products, arithmetic and copies ran while one was open for 1% -> 0% of each run, Pallas kernels for 0% -> 0%
where the time goes in v1:
time: 2360 us; the launch traced here: 2350 us
  waiting for transfers between devices  1930 us (82%)
  local copies, waits for them, and re-layouts  151 us (6%)
  blocking collectives  105 us (4%)
  other arithmetic  101 us (4%)
  matrix products  48.9 us (2%)
    all_gather x1, waiting for transfers between devices, expert_block(): gate_up = jnp.sum(lax.all_gather(gate_up, 'gy'), axis=0)  1890 us
    all_gather x2, blocking collectives, merged(): gathered = jax.tree.map(lambda a: lax.all_gather(a, axis), part)  73.9 us
    while x24, local copies, waits for them, and re-layouts  48.4 us
  transfers between devices with their start and end apart: 3, of which 3 were waited for; matrix products, arithmetic and copies ran while one was open for 0% of the time, Pallas kernels for 0%

profile of v1, /device:TPU:0, one launch (start us, length us, event | category | flops | bytes accessed | tf_op | source)
XLA Modules:
  0.0 2352.2 jit_solution(11346307846546142163)
XLA Ops:
  6.5 7.0 reshape.209
  13.6 7.0 reshape_squeeze.10
  22.4 178.0 %while.35 = (s32[]{:T(128)}, f32[64,4,5]{2,1,0:T(4,128)S(1)}, f32[64,4,5]{2,1,0:T(4,128)S(1)}, f32[64,4,5,128]{3,0,2,1:T(8,128)}, s32[8,512]{1,0:T(8,128)}, /*in...) while((s32[]{:T(128)}, f32[64,4,5]{2,1,0:T(4,128)S(1)}, ...), condition=%wide.region_3.4_spmd.clone, body=%wide.region_0.3_spmd.clone.sunk | while | flops 176462592 | bytes 21555320 | solution.py:98
  23.1 3.6 gather_fusion
  26.7 4.5 copy.169
  31.2 2.1 bitcast_convert_fusion.2
  34.9 2.3 multiply_reduce_fusion.4
  37.8 2.1 gather_fusion.1
  44.4 3.6 gather_fusion
  48.0 4.5 copy.169
  52.5 2.1 bitcast_convert_fusion.2
  56.2 2.3 multiply_reduce_fusion.4
  59.1 2.1 gather_fusion.1
  63.6 2.4 fusion.70
  66.8 3.6 gather_fusion
  70.4 4.5 copy.169
  74.9 2.1 bitcast_convert_fusion.2
  78.6 2.3 multiply_reduce_fusion.4
  81.5 2.1 gather_fusion.1
  86.0 2.4 fusion.70
  89.2 3.6 gather_fusion
  92.8 4.5 copy.169
  97.3 2.1 bitcast_convert_fusion.2
  101.0 2.3 multiply_reduce_fusion.4
  103.9 2.1 gather_fusion.1
  108.4 2.4 fusion.70
  111.6 3.6 gather_fusion
  115.2 4.5 copy.169
  119.7 2.1 bitcast_convert_fusion.2
  123.4 2.3 multiply_reduce_fusion.4
  126.3 2.1 gather_fusion.1
  130.8 2.4 fusion.70
  134.0 3.6 gather_fusion
  137.6 4.5 copy.169
  142.1 2.1 bitcast_convert_fusion.2
  145.8 2.3 multiply_reduce_fusion.4
  148.7 2.1 gather_fusion.1
  153.2 2.4 fusion.70
  156.4 3.6 gather_fusion
  160.0 4.5 copy.169
  164.5 2.1 bitcast_convert_fusion.2
  168.1 2.3 multiply_reduce_fusion.4
  171.1 2.1 gather_fusion.1
  175.6 2.4 fusion.70
  178.8 3.6 gather_fusion
  182.4 4.5 copy.169
  186.8 2.1 bitcast_convert_fusion.2
  190.5 2.3 multiply_reduce_fusion.4
  193.5 2.1 gather_fusion.1
  198.0 2.4 fusion.70
  202.2 38.6 %all-gather = f32[512,4,5]{2,1,0:T(4,128)S(1)} all-gather(f32[64,4,5]{2,1,0:T(4,128)S(1)} %get-tuple-element.232), channel_id=2, replica_groups=mesh['gx'=4,'gy'=8] {'gy'}, dimensions={0}, use_global_device_ids=true | all-gather | bytes 46080 | tf_op jit(solution)/shard_map/all_gather | solution.py:18
  240.9 35.2 %all-gather.1 = f32[512,4,5]{2,1,0:T(4,128)S(1)} all-gather(f32[64,4,5]{2,1,0:T(4,128)S(1)} %get-tuple-element.233), channel_id=3, replica_groups=mesh['gx'=4,'gy'=8] {'gy'}, dimensions={0}, use_global_device_ids=true | all-gather | bytes 46080 | tf_op jit(solution)/shard_map/all_gather | solution.py:18
  282.6 27.2 %all-gather.7.cloned.1.call-done = f32[512,4,5,128]{3,0,2,1:T(8,128)} async-done(((f32[64,4,5,128]{3,0,2,1:T(8,128)}), f32[512,4,5,128]{3,0,2,1:T(8,128)}) %all-gather.7.cloned.1.call-update) | async-done | bytes 5242896 | tf_op jit(solution)/shard_map/all_gather | solution.py:18
  311.4 20.6 while.34
  336.7 19.3 psum.7
  356.3 2.1 scatter_custom_fusion
  358.7 12.1 all_to_all.10
  370.8 16.6 fusion.23
  388.2 1891.7 %all-gather.9.cloned.1.call-done = f32[32,16,12,3072]{3,2,0,1:T(8,128)} async-done(((f32[4,16,12,3072]{3,2,0,1:T(8,128)}), f32[32,16,12,3072]{3,2,0,1:T(8,128)}) %all-gather.9.cloned.1.call-update) | async-done | bytes 75497488 | tf_op jit(solution)/shard_map/all_gather | solution.py:104
  2279.8 36.1 %reduce_sum.60 = f32[4,16,12,3072]{3,2,0,1:T(8,128)} reduce(f32[8,4,16,12,3072]{4,3,1,0,2:T(8,128)} %bitcast.12, f32[]{:T(128)} %constant.103.clone.1), dimensions={0}, to_apply=%region_14.15 | reduce | flops 16515072 | bytes 84934656 | tf_op jit(solution)/shard_map/reduce_sum | solution.py:104
  2316.0 11.6 fusion.34
  2328.8 3.5 all-to-all-start.1
  2332.5 9.2 all-to-all-done.1
  2342.2 2.1 gather_fusion.2
  (263 shorter events, 84.0 us)
Async XLA Ops:
  6.5 329.4 %copy-start = (bf16[2560,320]{0,1:T(8,128)(2,1)S(1)}, bf16[2560,320]{0,1:T(8,128)(2,1)}, u32[]{:S(2)}) copy-start(bf16[2560,320]{0,1:T(8,128)(2,1)} %param.21) | copy-start | bytes 4915204
  6.5 303.3 %all-gather.7.cloned.1.call-start = ((), (), s32[]{:S(2)}) async-start(), calls=%async_computation.2 | async-start | bytes 5898240 | tf_op jit(solution)/shard_map/all_gather | solution.py:18
  13.6 7.5 copy-start.7
  13.6 8.8 copy-start.2
  22.4 179.4 %copy-start.8 = (s32[256,6]{0,1:T(8,128)S(1)}, s32[256,6]{0,1:T(8,128)}, u32[]{:S(2)}) copy-start(s32[256,6]{0,1:T(8,128)} %param.24) | copy-start | bytes 18436
  200.4 78.9 %copy-start.4 = (bf16[64,1024]{1,0:T(8,128)(2,1)S(1)}, bf16[64,1024]{1,0:T(8,128)(2,1)}, u32[]{:S(2)}) copy-start(bf16[64,1024]{1,0:T(8,128)(2,1)} %param.17) | copy-start | bytes 393220
  200.5 80.5 %copy-start.9 = (bf16[320]{0:T(512)(128)(2,1)S(1)}, bf16[320]{0:T(512)(128)(2,1)}, u32[]{:S(2)}) copy-start(bf16[320]{0:T(512)(128)(2,1)} %param.23) | copy-start | bytes 1924
  200.5 2079.4 %all-gather.9.cloned.1.call-start = ((), (), s32[]{:S(2)}) async-start(), calls=%async_computation.3 | async-start | bytes 113246208 | tf_op jit(solution)/shard_map/all_gather | solution.py:104
  276.2 1.0 copy-start.3
  311.4 24.6 %copy-start.5 = (bf16[64,320]{1,0:T(8,128)(2,1)S(1)}, bf16[64,320]{1,0:T(8,128)(2,1)}, u32[]{:S(2)}) copy-start(bf16[64,320]{1,0:T(8,128)(2,1)} %param.22) | copy-start | bytes 122884
  387.4 0.7 copy-start.6
  2327.6 17.8 copy-start.1
  2328.8 13.0 all-to-all-start.1
Sparse Core Ops, SparseCore 0:
  200.6 109.1 all-gather.6
  387.6 1892.2 all-gather.8
